TPU v7x, 32 devices: a whole 2x2x4 slice. The times are simulated.
32 devices in a mesh: row: 2 (over y), col: 16 (over z, x, core).
Axes of the slice: x: 2, y: 2, z: 4, core: 2. Of those that a mesh axis runs over, the one named last changes fastest.
Arguments:
- blocks: bfloat16 [128, 2048, 128], P('row', 'col'), may hold values from -0.1875 to 0.1875
- block_rows: int32 [2, 1024], P('row', 'col'), may hold values from 0 to 2047, as said below
- block_cols: int32 [2, 1024], P('row', 'col'), may hold values from 0 to 255
- counts: int32 [2, 16], P('row', 'col'), may hold values from 1 to 64, as said below
- start_vectors: float32 [32, 524288], P(None, ('row', 'col')), may hold values from -6 to 6
Outputs:
- vectors: float32 [32, 524288], P(None, ('row', 'col'))
Inputs may be any that keep to these rules, and one draw needn't show every extreme that they name: counts[r, c] is the number of live slots of grid position (r, c); in every draw some position has all 64 slots live. For every grid position (r, c) and every o < 16, exactly 4 of its 64 slots have block_rows[r, c * 64 + s] // 128 == o.
All inputs are finite; a program needn't handle non-finite values.
Results may differ from a plain program's by a relative error of at most 0.0036.
Values may be sent and summed in bfloat16 or wider, within the bound.
A program may use at most 256 MiB of HBM per device.

v0:
```python
import math
import jax
import jax.numpy as jnp
from jax import lax
from jax.sharding import PartitionSpec as P

N = 524288
ITERS = 2


def cholesky_lower(gram_matrix):
    matrix_order = gram_matrix.shape[0]
    positions = jnp.arange(matrix_order)

    def column_step(position, factor):
        before = (positions < position).astype(gram_matrix.dtype)
        target_row = lax.dynamic_index_in_dim(factor, position, 0, keepdims=False) * before
        column = lax.dynamic_index_in_dim(gram_matrix, position, 1, keepdims=False)
        residue = column - jnp.sum(factor * target_row[None, :], axis=1)
        on_diagonal = positions == position
        pivot_value = jnp.sqrt(jnp.sum(jnp.where(on_diagonal, residue, 0.0)))
        values = jnp.where(on_diagonal, pivot_value, residue / pivot_value)
        values = jnp.where(positions >= position, values, 0.0)
        return lax.dynamic_update_index_in_dim(factor, values, position, 1)

    return lax.fori_loop(0, matrix_order, column_step, jnp.zeros_like(gram_matrix))


def lower_inverse(lower_factor):
    matrix_order = lower_factor.shape[0]
    positions = jnp.arange(matrix_order)

    def row_step(position, inverse):
        lower_row = lax.dynamic_index_in_dim(lower_factor, position, 0, keepdims=False)
        before = (positions < position).astype(lower_factor.dtype)
        inner_sum = jnp.sum((lower_row * before)[:, None] * inverse, axis=0)
        unit_row = (positions == position).astype(lower_factor.dtype)
        pivot_value = jnp.sum(lower_row * unit_row)
        return lax.dynamic_update_index_in_dim(
            inverse, (unit_row - inner_sum) / pivot_value, position, 0
        )

    return lax.fori_loop(0, matrix_order, row_step, jnp.zeros_like(lower_factor))


def accumulate(blocks, rows_index, cols_index, live_count, row_panel, col_panel):
    slot_count, block_size = (blocks.shape[0], blocks.shape[1])
    vector_count = row_panel.shape[0]
    row_blocks = row_panel.reshape(vector_count, -1, block_size)
    col_blocks = col_panel.reshape(vector_count, -1, block_size)
    group_size = math.gcd(slot_count, 64)
    turn_count = (live_count + group_size - 1) // group_size
    slot_offsets = jnp.arange(group_size, dtype=jnp.int32)

    def one_group(turn_index, partial_sums):
        row_sums, col_sums = partial_sums
        first_slot = turn_index * group_size
        live_mask = (first_slot + slot_offsets < live_count).astype(jnp.float32)
        from_cols = jnp.take(col_blocks, cols_index, axis=1)
        from_rows = jnp.take(row_blocks, rows_index, axis=1)
        to_cols = jnp.einsum("kgi,gij->kgj", from_rows, blocks, preferred_element_type=jnp.float32)
        col_sums = col_sums.at[:, cols_index].add(to_cols * live_mask[None, :, None])
        to_rows = jnp.einsum("kgj,gij->kgi", from_cols, blocks, preferred_element_type=jnp.float32)
        row_sums = row_sums.at[:, rows_index].add(to_rows * live_mask[None, :, None])
        return (row_sums, col_sums)

    row_start = jnp.zeros(row_blocks.shape, jnp.float32)
    initial = (row_start, jnp.zeros(col_blocks.shape, jnp.float32))
    return lax.fori_loop(0, turn_count, one_group, initial)


def per_device(blocks, block_rows, block_cols, counts, start_vectors):
    live_count = counts[0, 0]
    rows_index = block_rows[0]
    cols_index = block_cols[0]
    vectors = start_vectors
    for iteration in range(ITERS):
        rounded = vectors.astype(jnp.bfloat16)
        vector_count = rounded.shape[0]
        col_panel = lax.all_gather(rounded, "row", axis=1, tiled=True)
        row_panel = lax.all_gather(rounded, "col", axis=1, tiled=True)
        row_sums, col_sums = accumulate(
            blocks, rows_index, cols_index, live_count, row_panel, col_panel
        )
        from_row_group = lax.psum_scatter(
            row_sums.reshape(vector_count, -1), "col", scatter_dimension=1, tiled=True
        )
        from_col_group = lax.psum_scatter(
            col_sums.reshape(vector_count, -1), "row", scatter_dimension=1, tiled=True
        )
        product = from_row_group + from_col_group
        local_gram = jnp.dot(
            product, product.T, precision=lax.Precision.HIGHEST, preferred_element_type=jnp.float32
        )
        gram_matrix = lax.psum(local_gram, ("row", "col")) / N
        inverse = lower_inverse(cholesky_lower(gram_matrix))
        vectors = jnp.dot(
            inverse, product, precision=lax.Precision.HIGHEST, preferred_element_type=jnp.float32
        )
    return vectors


def solution(mesh):
    placed = (
        P("row", "col", None),
        P("row", "col"),
        P("row", "col"),
        P("row", "col"),
        P(None, ("row", "col")),
    )
    return jax.shard_map(
        per_device, mesh=mesh, in_specs=placed, out_specs=P(None, ("row", "col")), check_vma=False
    )
```

profile of v0, /device:TPU:0, one launch (start us, length us, event | category | flops | bytes accessed | tf_op | source)
XLA Modules:
  0.0 1549.7 jit_solution(5209276909103308987)
XLA Ops:
  6.5 2.8 convert_element_type.66
  11.0 34.4 %all-gather.5.cloned.1.call-done = bf16[32,32768]{1,0:T(8,128)(2,1)} async-done(((bf16[32,16384]{1,0:T(8,128)(2,1)}), bf16[32,32768]{1,0:T(8,128)(2,1)}) %all-gather.5.cloned.1.call-update) | async-done | bytes 2097168 | tf_op jit(solution)/shard_map/all_gather | solution.py:80
  45.4 3.3 copy_bitcast_fusion.7
  48.6 2.2 gather_fusion
  50.9 2.2 fusion.34
  53.1 121.4 %all-gather.7.cloned.1.call-done = bf16[32,262144]{1,0:T(8,128)(2,1)} async-done(((bf16[32,16384]{1,0:T(8,128)(2,1)}), bf16[32,262144]{1,0:T(8,128)(2,1)}) %all-gather.7.cloned.1.call-update) | async-done | bytes 16777232 | tf_op jit(solution)/shard_map/all_gather | solution.py:81
  174.5 14.5 copy_bitcast_fusion.3
  189.0 6.4 gather_fusion.1
  195.4 1.7 fusion.32
  197.1 11.3 broadcast.314.clone
  208.4 2.6 broadcast.315.clone
  210.9 20.4 %while.90 = (s32[]{:T(128)}, f32[32,2048,128]{2,0,1:T(8,128)}, f32[32,256,128]{2,0,1:T(8,128)}, s32[]{:T(128)}, s32[64]{0:T(128)S(1)}, /*index=5*/s32[]{:T(128)}...) while((s32[]{:T(128)}, f32[32,2048,128]{2,0,1:T(8,128)}, ...), condition=%wide.region_3.6_spmd.clone, body=%wide.region_0.5_spmd.clone.sunk | while | flops 1049155 | bytes 10487937 | solution.py:69
  211.6 2.7 broadcast_multiply_fusion.8
  214.3 9.0 scatter_fusion
  223.3 8.0 scatter_fusion.1
  231.3 4.4 copy_bitcast_fusion.5
  235.8 22.6 %copy_bitcast_fusion.1 = f32[32,262144]{1,0:T(8,128)} fusion(f32[32,2048,128]{2,0,1:T(8,128)} %get-tuple-element.609), kind=kLoop, calls=%fused_computation.69 | loop fusion | bytes 67108864 | tf_op jit(solution)/shard_map/reshape | solution.py:86
  258.5 30.0 %reduce-scatter.7.cloned.1.call-done = f32[32,16384]{1,0:T(8,128)} async-done(((f32[32,32768]{1,0:T(8,128)}), f32[32,16384]{1,0:T(8,128)}) %reduce-scatter.7.cloned.1.call-update) | async-done | bytes 2097168 | tf_op jit(solution)/shard_map/reduce_scatter | solution.py:88
  288.4 337.4 %reduce-scatter.5.cloned.1.call-done = f32[32,16384]{1,0:T(8,128)} async-done(((f32[32,262144]{1,0:T(8,128)}), f32[32,16384]{1,0:T(8,128)}) %reduce-scatter.5.cloned.1.call-update) | async-done | bytes 2097168 | tf_op jit(solution)/shard_map/reduce_scatter | solution.py:85
  625.8 2.4 add.220
  629.5 1.8 fusion.52
  631.3 39.1 %psum.14 = f32[32,32]{1,0:T(8,128)S(1)} all-reduce(f32[32,32]{1,0:T(8,128)S(1)} %fusion.52), channel_id=1, replica_groups=mesh['row'=2,'col'=16] {'row','col'}, use_global_device_ids=true, to_apply=%region_6.9 | all-reduce | flops 1024 | bytes 8192 | tf_op jit(solution)/shard_map/psum | solution.py:95
  670.4 58.1 %while.92 = (s32[]{:T(128)}, f32[32,32]{1,0:T(8,128)S(1)}, f32[32,32]{0,1:T(8,128)S(1)}, s32[]{:T(128)}, s32[]{:T(128)}) while((s32[]{:T(128)}, f32[32,32]{1,0:T(8,128)S(1)}, f32[32,32]{0,1:T(8,128)S(1)}, s32[]{:T(128)}, s32[]{:T(128)}) %tuple.192), condition=%wide.region_10.13_spmd.clone.clone, body=%wide.region_7.12_spmd.clone.clone.sunk | while | flops 2401 | bytes 8913 | solution.py:26
  728.6 49.0 %while.93 = (s32[]{:T(128)}, f32[32,32]{1,0:T(8,128)S(1)}, f32[32,32]{1,0:T(8,128)S(1)}, s32[]{:T(128)}, s32[]{:T(128)}) while((s32[]{:T(128)}, f32[32,32]{1,0:T(8,128)S(1)}, f32[32,32]{1,0:T(8,128)S(1)}, s32[]{:T(128)}, s32[]{:T(128)}) %tuple.195), condition=%wide.region_14.17_spmd.clone.clone, body=%wide.region_11.16_spmd.clone.clone.sunk | while | flops 2305 | bytes 6221 | solution.py:43
  777.6 4.4 convolution_convert_fusion
  782.8 32.2 %all-gather.9.cloned.1.call-done = bf16[32,32768]{1,0:T(8,128)(2,1)} async-done(((bf16[32,16384]{1,0:T(8,128)(2,1)}), bf16[32,32768]{1,0:T(8,128)(2,1)}) %all-gather.9.cloned.1.call-update) | async-done | bytes 2097168 | tf_op jit(solution)/shard_map/all_gather | solution.py:80
  815.1 3.3 copy_bitcast_fusion.6
  818.3 2.2 gather_fusion.2
  820.6 2.2 fusion.30
  822.8 121.5 %all-gather.11.cloned.1.call-done = bf16[32,262144]{1,0:T(8,128)(2,1)} async-done(((bf16[32,16384]{1,0:T(8,128)(2,1)}), bf16[32,262144]{1,0:T(8,128)(2,1)}) %all-gather.11.cloned.1.call-update) | async-done | bytes 16777232 | tf_op jit(solution)/shard_map/all_gather | solution.py:81
  944.3 14.5 copy_bitcast_fusion.2
  958.8 6.4 gather_fusion.3
  966.9 11.3 broadcast.314
  978.2 2.6 broadcast.315
  980.7 20.4 %while.91 = (s32[]{:T(128)}, f32[32,2048,128]{2,0,1:T(8,128)}, f32[32,256,128]{2,0,1:T(8,128)}, s32[]{:T(128)}, s32[64]{0:T(128)S(1)}, /*index=5*/s32[]{:T(128)}...) while((s32[]{:T(128)}, f32[32,2048,128]{2,0,1:T(8,128)}, ...), condition=%wide.region_18.21_spmd.clone, body=%wide.region_15.20_spmd.clone.sunk | while | flops 1049155 | bytes 10487937 | solution.py:69
  981.4 2.7 broadcast_multiply_fusion.9
  984.1 9.0 scatter_fusion.2
  993.1 8.0 scatter_fusion.3
  1001.1 4.4 copy_bitcast_fusion.4
  1005.6 22.6 %copy_bitcast_fusion = f32[32,262144]{1,0:T(8,128)} fusion(f32[32,2048,128]{2,0,1:T(8,128)} %get-tuple-element.613), kind=kLoop, calls=%fused_computation.68 | loop fusion | bytes 67108864 | tf_op jit(solution)/shard_map/reshape | solution.py:86
  1028.2 30.0 %reduce-scatter.11.cloned.1.call-done = f32[32,16384]{1,0:T(8,128)} async-done(((f32[32,32768]{1,0:T(8,128)}), f32[32,16384]{1,0:T(8,128)}) %reduce-scatter.11.cloned.1.call-update) | async-done | bytes 2097168 | tf_op jit(solution)/shard_map/reduce_scatter | solution.py:88
  1058.2 336.9 %reduce-scatter.9.cloned.1.call-done = f32[32,16384]{1,0:T(8,128)} async-done(((f32[32,262144]{1,0:T(8,128)}), f32[32,16384]{1,0:T(8,128)}) %reduce-scatter.9.cloned.1.call-update) | async-done | bytes 2097168 | tf_op jit(solution)/shard_map/reduce_scatter | solution.py:85
  1395.2 2.4 add.221
  1398.9 1.8 fusion.53
  1400.7 39.0 %psum.15 = f32[32,32]{1,0:T(8,128)S(1)} all-reduce(f32[32,32]{1,0:T(8,128)S(1)} %fusion.53), channel_id=1, replica_groups=mesh['row'=2,'col'=16] {'row','col'}, use_global_device_ids=true, to_apply=%region_21.24 | all-reduce | flops 1024 | bytes 8192 | tf_op jit(solution)/shard_map/psum | solution.py:95
  1439.8 53.9 %while.94 = (s32[]{:T(128)}, f32[32,32]{1,0:T(8,128)S(1)}, f32[32,32]{0,1:T(8,128)S(1)}, s32[]{:T(128)}, s32[]{:T(128)}) while((s32[]{:T(128)}, f32[32,32]{1,0:T(8,128)S(1)}, f32[32,32]{0,1:T(8,128)S(1)}, s32[]{:T(128)}, s32[]{:T(128)}) %tuple.201), condition=%wide.region_25.28_spmd.clone.clone, body=%wide.region_22.27_spmd.clone.clone.sunk | while | flops 2401 | bytes 8913 | solution.py:26
  1493.7 44.3 %while.95 = (s32[]{:T(128)}, f32[32,32]{1,0:T(8,128)S(1)}, f32[32,32]{1,0:T(8,128)S(1)}, s32[]{:T(128)}, s32[]{:T(128)}) while((s32[]{:T(128)}, f32[32,32]{1,0:T(8,128)S(1)}, f32[32,32]{1,0:T(8,128)S(1)}, s32[]{:T(128)}, s32[]{:T(128)}) %tuple.204), condition=%wide.region_29.32_spmd.clone.clone, body=%wide.region_26.31_spmd.clone.clone.sunk | while | flops 2305 | bytes 6221 | solution.py:43
  1538.1 4.8 fusion.54
  (685 shorter events, 164.6 us)
Async XLA Ops:
  6.5 44.4 %copy-start = (bf16[64,128,128]{2,1,0:T(8,128)(2,1)S(1)}, bf16[64,128,128]{2,1,0:T(8,128)(2,1)}, u32[]{:S(2)}) copy-start(bf16[64,128,128]{2,1,0:T(8,128)(2,1)} %param.21) | copy-start | bytes 6291460
  6.5 4.3 copy-start.3
  6.5 4.4 copy-start.4
  6.5 38.8 %all-gather.5.cloned.1.call-start = ((), (), s32[]{:S(2)}) async-start(), calls=%async_computation.4 | async-start | bytes 3145728 | tf_op jit(solution)/shard_map/all_gather | solution.py:80
  9.4 165.1 %all-gather.7.cloned.1.call-start = ((), (), s32[]{:S(2)}) async-start(), calls=%async_computation.5 | async-start | bytes 17825792 | tf_op jit(solution)/shard_map/all_gather | solution.py:81
  10.2 278.3 %reduce-scatter.7.cloned.1.call-start = ((), (), s32[]{:S(2)}) async-start(), calls=%async_computation.7 | async-start | bytes 6291456 | tf_op jit(solution)/shard_map/reduce_scatter | solution.py:88
  235.8 390.0 %reduce-scatter.5.cloned.1.call-start = ((), (), s32[]{:S(2)}) async-start(), calls=%async_computation.6 | async-start | bytes 35651584 | tf_op jit(solution)/shard_map/reduce_scatter | solution.py:85
  258.4 556.7 %all-gather.9.cloned.1.call-start = ((), (), s32[]{:S(2)}) async-start(), calls=%async_computation.8 | async-start | bytes 3145728 | tf_op jit(solution)/shard_map/all_gather | solution.py:80
  628.2 1.3 copy-start.2
  782.0 162.3 %all-gather.11.cloned.1.call-start = ((), (), s32[]{:S(2)}) async-start(), calls=%async_computation.9 | async-start | bytes 17825792 | tf_op jit(solution)/shard_map/all_gather | solution.py:81
  782.6 275.6 %reduce-scatter.11.cloned.1.call-start = ((), (), s32[]{:S(2)}) async-start(), calls=%async_computation.11 | async-start | bytes 6291456 | tf_op jit(solution)/shard_map/reduce_scatter | solution.py:88
  1005.6 389.6 %reduce-scatter.9.cloned.1.call-start = ((), (), s32[]{:S(2)}) async-start(), calls=%async_computation.10 | async-start | bytes 35651584 | tf_op jit(solution)/shard_map/reduce_scatter | solution.py:85
  1397.6 1.4 copy-start.1
Sparse Core Ops, SparseCore 0:
  9.5 35.8 all-gather.4
  47.6 126.9 all-gather.6
  235.9 52.4 reduce-scatter.6
  293.1 332.6 reduce-scatter.4
  782.1 32.8 all-gather.8
  817.4 126.9 all-gather.10
  1005.7 52.4 reduce-scatter.10
  1062.5 332.6 reduce-scatter.8
where the time goes:
time: 1550 us
  waiting for transfers between devices  1050 us (68%)
  other arithmetic  189 us (12%)
  local copies, waits for them, and re-layouts  153 us (10%)
  blocking collectives  78.1 us (5%)
  loops' own time  48.3 us (3%)
  matrix products  20.5 us (1%)
    reduce_scatter x2, waiting for transfers between devices, per_device(): lax.psum_scatter(row_sums.reshape(vector_count, -1), 'col', scatter_dimen...  674 us
    all_gather x2, waiting for transfers between devices, per_device(): row_panel = lax.all_gather(rounded, 'col', axis=1, tiled=True)  243 us
    psum x2, blocking collectives, per_device(): gram_matrix = lax.psum(local_gram, ('row', 'col')) / N  78.1 us
    all_gather x2, waiting for transfers between devices, per_device(): col_panel = lax.all_gather(rounded, 'row', axis=1, tiled=True)  66.7 us
    reduce_scatter x2, waiting for transfers between devices, per_device(): lax.psum_scatter(col_sums.reshape(vector_count, -1), 'row', scatter_dimen...  60 us
    another operation x2, loops' own time, cholesky_lower(): lax.fori_loop(0, matrix_order, column_step, jnp.zeros_like(gram_matrix))  46.9 us
    reshape x2, local copies, waits for them, and re-layouts, per_device(): row_sums.reshape(vector_count, -1)  45.2 us
    reduce_sum x64, other arithmetic, column_step(): pivot_value = jnp.sqrt(jnp.sum(jnp.where(on_diagonal, residue, 0.0)))  42.8 us
  transfers between devices with their start and end apart: 8, of which 8 were waited for; matrix products, arithmetic and copies ran while one was open for 4% of the time, Pallas kernels for 0%

commit v1 on v0

--- a/solution.py
+++ b/solution.py
@@ -77,7 +77,22 @@
     for iteration in range(ITERS):
         rounded = vectors.astype(jnp.bfloat16)
         vector_count = rounded.shape[0]
-        col_panel = lax.all_gather(rounded, "row", axis=1, tiled=True)
+        z_new, base_arr, b_next = (lax.axis_size("row"), lax.axis_index("row"), rounded.shape[1])
+        earlier, field_out = (rounded, 1)
+        while field_out < z_new:
+            earlier = jnp.concatenate(
+                [
+                    earlier,
+                    lax.ppermute(
+                        earlier,
+                        axis_name="row",
+                        perm=[(rr, (rr - field_out) % z_new) for rr in range(z_new)],
+                    ),
+                ],
+                axis=1,
+            )
+            field_out = 2 * field_out
+        col_panel = jnp.roll(earlier, base_arr * b_next, axis=1)
         row_panel = lax.all_gather(rounded, "col", axis=1, tiled=True)
         row_sums, col_sums = accumulate(
             blocks, rows_index, cols_index, live_count, row_panel, col_panel

time: 1550 us -> 1480 us (0.955)
  waiting for transfers between devices: 1050 us -> 960 us
  other arithmetic: 189 us -> 205 us
    all_gather x2 -> x0, waiting for transfers between devices: 66.7 us -> none  [per_device(): col_panel = lax.all_gather(rounded, 'row', axis=1, tiled=True)]
    all_gather x2, waiting for transfers between devices: 243 us -> 181 us  [per_device(): row_panel = lax.all_gather(rounded, 'col', axis=1, tiled=True)]
    ppermute x0 -> x2, waiting for transfers between devices: none -> 44.6 us  [per_device(): lax.ppermute(earlier, axis_name='row', perm=[(rr, (rr - field_out) % z_ne...]
    reshape x0 -> x2, other arithmetic: none -> 15.9 us  [accumulate(): col_blocks = col_panel.reshape(vector_count, -1, block_size)]
  transfers between devices with their start and end apart: 8 -> 8, of which waited for: 8 -> 8; matrix products, arithmetic and copies ran while one was open for 4% -> 5% of each run, Pallas kernels for 0% -> 0%
where the time goes in v1:
time: 1480 us
  waiting for transfers between devices  960 us (65%)
  other arithmetic  205 us (14%)
  local copies, waits for them, and re-layouts  147 us (10%)
  blocking collectives  78.2 us (5%)
  loops' own time  48.3 us (3%)
  matrix products  20.5 us (1%)
    reduce_scatter x2, waiting for transfers between devices, per_device(): lax.psum_scatter(row_sums.reshape(vector_count, -1), 'col', scatter_dimen...  674 us
    all_gather x2, waiting for transfers between devices, per_device(): row_panel = lax.all_gather(rounded, 'col', axis=1, tiled=True)  181 us
    psum x2, blocking collectives, per_device(): gram_matrix = lax.psum(local_gram, ('row', 'col')) / N  78.2 us
    reduce_scatter x2, waiting for transfers between devices, per_device(): lax.psum_scatter(col_sums.reshape(vector_count, -1), 'row', scatter_dimen...  59.7 us
    another operation x2, loops' own time, cholesky_lower(): lax.fori_loop(0, matrix_order, column_step, jnp.zeros_like(gram_matrix))  46.9 us
    reshape x2, local copies, waits for them, and re-layouts, per_device(): row_sums.reshape(vector_count, -1)  45.2 us
    ppermute x2, waiting for transfers between devices, per_device(): lax.ppermute(earlier, axis_name='row', perm=[(rr, (rr - field_out) % z_ne...  44.6 us
    reduce_sum x64, other arithmetic, column_step(): pivot_value = jnp.sqrt(jnp.sum(jnp.where(on_diagonal, residue, 0.0)))  42.8 us
  transfers between devices with their start and end apart: 8, of which 8 were waited for; matrix products, arithmetic and copies ran while one was open for 5% of the time, Pallas kernels for 0%

profile of v1, /device:TPU:0, one launch (start us, length us, event | category | flops | bytes accessed | tf_op | source)
XLA Modules:
  0.0 1479.2 jit_solution(17562794134432505275)
XLA Ops:
  6.5 2.8 convert_element_type.66
  9.5 3.0 collective-permute-start
  13.3 22.6 %collective-permute-done = bf16[32,16384]{1,0:T(8,128)(2,1)S(1)} collective-permute-done((bf16[32,16384]{1,0:T(8,128)(2,1)}, bf16[32,16384]{1,0:T(8,128)(2,1)S(1)}, u32[]{:S(2)}, u32[]{:S(2)}) %collective-permute-start) | collective-permute-done | bytes 1048608 | tf_op jit(solution)/shard_map/ppermute | solution.py:86
  35.9 7.9 copy_bitcast_fusion.7
  43.8 2.3 gather_fusion
  46.1 2.2 fusion.42
  48.3 90.9 %all-gather.3.cloned.1.call-done = bf16[32,262144]{1,0:T(8,128)(2,1)} async-done(((bf16[32,16384]{1,0:T(8,128)(2,1)}), bf16[32,262144]{1,0:T(8,128)(2,1)}) %all-gather.3.cloned.1.call-update) | async-done | bytes 16777232 | tf_op jit(solution)/shard_map/all_gather | solution.py:96
  139.2 14.5 copy_bitcast_fusion.3
  153.7 6.4 gather_fusion.1
  161.8 11.3 broadcast.315.clone
  173.1 2.6 broadcast.316.clone
  175.6 20.4 %while.90 = (s32[]{:T(128)}, f32[32,2048,128]{2,0,1:T(8,128)}, f32[32,256,128]{2,0,1:T(8,128)}, s32[]{:T(128)}, s32[64]{0:T(128)S(1)}, /*index=5*/s32[]{:T(128)}...) while((s32[]{:T(128)}, f32[32,2048,128]{2,0,1:T(8,128)}, ...), condition=%wide.region_3.7_spmd.clone, body=%wide.region_0.6_spmd.clone.sunk | while | flops 1049155 | bytes 10487937 | solution.py:69
  176.3 2.7 broadcast_multiply_fusion.8
  179.0 9.0 scatter_fusion
  188.0 8.0 scatter_fusion.1
  196.0 4.4 copy_bitcast_fusion.5
  200.5 22.6 %copy_bitcast_fusion.1 = f32[32,262144]{1,0:T(8,128)} fusion(f32[32,2048,128]{2,0,1:T(8,128)} %get-tuple-element.610), kind=kLoop, calls=%fused_computation.69 | loop fusion | bytes 67108864 | tf_op jit(solution)/shard_map/reshape | solution.py:101
  223.2 30.0 %reduce-scatter.7.cloned.1.call-done = f32[32,16384]{1,0:T(8,128)} async-done(((f32[32,32768]{1,0:T(8,128)}), f32[32,16384]{1,0:T(8,128)}) %reduce-scatter.7.cloned.1.call-update) | async-done | bytes 2097168 | tf_op jit(solution)/shard_map/reduce_scatter | solution.py:103
  253.1 337.7 %reduce-scatter.5.cloned.1.call-done = f32[32,16384]{1,0:T(8,128)} async-done(((f32[32,262144]{1,0:T(8,128)}), f32[32,16384]{1,0:T(8,128)}) %reduce-scatter.5.cloned.1.call-update) | async-done | bytes 2097168 | tf_op jit(solution)/shard_map/reduce_scatter | solution.py:100
  590.8 2.4 add.228
  594.6 1.8 fusion.60
  596.3 39.2 %psum.14 = f32[32,32]{1,0:T(8,128)S(1)} all-reduce(f32[32,32]{1,0:T(8,128)S(1)} %fusion.60), channel_id=1, replica_groups=mesh['row'=2,'col'=16] {'row','col'}, use_global_device_ids=true, to_apply=%region_6.10 | all-reduce | flops 1024 | bytes 8192 | tf_op jit(solution)/shard_map/psum | solution.py:110
  635.6 58.1 %while.92 = (s32[]{:T(128)}, f32[32,32]{1,0:T(8,128)S(1)}, f32[32,32]{0,1:T(8,128)S(1)}, s32[]{:T(128)}, s32[]{:T(128)}) while((s32[]{:T(128)}, f32[32,32]{1,0:T(8,128)S(1)}, f32[32,32]{0,1:T(8,128)S(1)}, s32[]{:T(128)}, s32[]{:T(128)}) %tuple.194), condition=%wide.region_10.14_spmd.clone.clone, body=%wide.region_7.13_spmd.clone.clone.sunk | while | flops 2401 | bytes 8913 | solution.py:26
  693.7 48.9 %while.93 = (s32[]{:T(128)}, f32[32,32]{1,0:T(8,128)S(1)}, f32[32,32]{1,0:T(8,128)S(1)}, s32[]{:T(128)}, s32[]{:T(128)}) while((s32[]{:T(128)}, f32[32,32]{1,0:T(8,128)S(1)}, f32[32,32]{1,0:T(8,128)S(1)}, s32[]{:T(128)}, s32[]{:T(128)}) %tuple.197), condition=%wide.region_14.18_spmd.clone.clone, body=%wide.region_11.17_spmd.clone.clone.sunk | while | flops 2305 | bytes 6221 | solution.py:43
  742.7 4.4 convolution_convert_fusion
  747.2 2.4 collective-permute-start.1
  749.6 22.0 %collective-permute-done.1 = bf16[32,16384]{1,0:T(8,128)(2,1)S(1)} collective-permute-done((bf16[32,16384]{1,0:T(8,128)(2,1)}, bf16[32,16384]{1,0:T(8,128)(2,1)S(1)}, u32[]{:S(2)}, u32[]{:S(2)}) %collective-permute-start.1) | collective-permute-done | bytes 1048608 | tf_op jit(solution)/shard_map/ppermute | solution.py:86
  771.6 7.9 copy_bitcast_fusion.6
  779.5 2.2 gather_fusion.2
  781.8 2.2 fusion.38
  784.0 90.0 %all-gather.5.cloned.1.call-done = bf16[32,262144]{1,0:T(8,128)(2,1)} async-done(((bf16[32,16384]{1,0:T(8,128)(2,1)}), bf16[32,262144]{1,0:T(8,128)(2,1)}) %all-gather.5.cloned.1.call-update) | async-done | bytes 16777232 | tf_op jit(solution)/shard_map/all_gather | solution.py:96
  874.0 14.5 copy_bitcast_fusion.2
  888.5 6.4 gather_fusion.3
  896.6 11.3 broadcast.315
  907.9 2.6 broadcast.316
  910.4 20.4 %while.91 = (s32[]{:T(128)}, f32[32,2048,128]{2,0,1:T(8,128)}, f32[32,256,128]{2,0,1:T(8,128)}, s32[]{:T(128)}, s32[64]{0:T(128)S(1)}, /*index=5*/s32[]{:T(128)}...) while((s32[]{:T(128)}, f32[32,2048,128]{2,0,1:T(8,128)}, ...), condition=%wide.region_18.22_spmd.clone, body=%wide.region_15.21_spmd.clone.sunk | while | flops 1049155 | bytes 10487937 | solution.py:69
  911.1 2.7 broadcast_multiply_fusion.9
  913.8 9.0 scatter_fusion.2
  922.8 8.0 scatter_fusion.3
  930.8 4.4 copy_bitcast_fusion.4
  935.5 22.6 %copy_bitcast_fusion = f32[32,262144]{1,0:T(8,128)} fusion(f32[32,2048,128]{2,0,1:T(8,128)} %get-tuple-element.614), kind=kLoop, calls=%fused_computation.68 | loop fusion | bytes 67108864 | tf_op jit(solution)/shard_map/reshape | solution.py:101
  958.1 29.8 %reduce-scatter.11.cloned.1.call-done = f32[32,16384]{1,0:T(8,128)} async-done(((f32[32,32768]{1,0:T(8,128)}), f32[32,16384]{1,0:T(8,128)}) %reduce-scatter.11.cloned.1.call-update) | async-done | bytes 2097168 | tf_op jit(solution)/shard_map/reduce_scatter | solution.py:103
  987.9 336.8 %reduce-scatter.9.cloned.1.call-done = f32[32,16384]{1,0:T(8,128)} async-done(((f32[32,262144]{1,0:T(8,128)}), f32[32,16384]{1,0:T(8,128)}) %reduce-scatter.9.cloned.1.call-update) | async-done | bytes 2097168 | tf_op jit(solution)/shard_map/reduce_scatter | solution.py:100
  1324.7 2.4 add.229
  1330.3 39.0 %psum.15 = f32[32,32]{1,0:T(8,128)S(1)} all-reduce(f32[32,32]{1,0:T(8,128)S(1)} %fusion.61), channel_id=1, replica_groups=mesh['row'=2,'col'=16] {'row','col'}, use_global_device_ids=true, to_apply=%region_21.25 | all-reduce | flops 1024 | bytes 8192 | tf_op jit(solution)/shard_map/psum | solution.py:110
  1369.4 53.9 %while.94 = (s32[]{:T(128)}, f32[32,32]{1,0:T(8,128)S(1)}, f32[32,32]{0,1:T(8,128)S(1)}, s32[]{:T(128)}, s32[]{:T(128)}) while((s32[]{:T(128)}, f32[32,32]{1,0:T(8,128)S(1)}, f32[32,32]{0,1:T(8,128)S(1)}, s32[]{:T(128)}, s32[]{:T(128)}) %tuple.203), condition=%wide.region_25.29_spmd.clone.clone, body=%wide.region_22.28_spmd.clone.clone.sunk | while | flops 2401 | bytes 8913 | solution.py:26
  1423.3 44.3 %while.95 = (s32[]{:T(128)}, f32[32,32]{1,0:T(8,128)S(1)}, f32[32,32]{1,0:T(8,128)S(1)}, s32[]{:T(128)}, s32[]{:T(128)}) while((s32[]{:T(128)}, f32[32,32]{1,0:T(8,128)S(1)}, f32[32,32]{1,0:T(8,128)S(1)}, s32[]{:T(128)}, s32[]{:T(128)}) %tuple.206), condition=%wide.region_29.33_spmd.clone.clone, body=%wide.region_26.32_spmd.clone.clone.sunk | while | flops 2305 | bytes 6221 | solution.py:43
  1467.6 4.8 fusion.62
  (682 shorter events, 166.8 us)
Async XLA Ops:
  6.5 39.5 %copy-start = (bf16[64,128,128]{2,1,0:T(8,128)(2,1)S(1)}, bf16[64,128,128]{2,1,0:T(8,128)(2,1)}, u32[]{:S(2)}) copy-start(bf16[64,128,128]{2,1,0:T(8,128)(2,1)} %param.23) | copy-start | bytes 6291460
  6.5 6.6 copy-start.4
  6.5 6.7 copy-start.3
  6.5 132.7 %all-gather.3.cloned.1.call-start = ((), (), s32[]{:S(2)}) async-start(), calls=%async_computation.4 | async-start | bytes 17825792 | tf_op jit(solution)/shard_map/all_gather | solution.py:96
  9.4 243.7 %reduce-scatter.7.cloned.1.call-start = ((), (), s32[]{:S(2)}) async-start(), calls=%async_computation.6 | async-start | bytes 6291456 | tf_op jit(solution)/shard_map/reduce_scatter | solution.py:103
  9.5 26.4 %collective-permute-start = (bf16[32,16384]{1,0:T(8,128)(2,1)}, bf16[32,16384]{1,0:T(8,128)(2,1)S(1)}, u32[]{:S(2)}, u32[]{:S(2)}) collective-permute-start(bf16[32,16384]{1,0:T(8,128)(2,1)} %convert_element_type.66), channel_id=1, source_target_pairs={{0,16},{16,0},{1,17},{17,1},{2,18},{18,2},{3,19},{19,3},{4,20},{20... | collective-permute-start | bytes 3145736 | tf_op jit(solution)/shard_map/ppermute | solution.py:86
  200.5 390.3 %reduce-scatter.5.cloned.1.call-start = ((), (), s32[]{:S(2)}) async-start(), calls=%async_computation.5 | async-start | bytes 35651584 | tf_op jit(solution)/shard_map/reduce_scatter | solution.py:100
  223.1 650.9 %all-gather.5.cloned.1.call-start = ((), (), s32[]{:S(2)}) async-start(), calls=%async_computation.7 | async-start | bytes 17825792 | tf_op jit(solution)/shard_map/all_gather | solution.py:96
  593.2 1.3 copy-start.2
  747.2 240.8 %reduce-scatter.11.cloned.1.call-start = ((), (), s32[]{:S(2)}) async-start(), calls=%async_computation.9 | async-start | bytes 6291456 | tf_op jit(solution)/shard_map/reduce_scatter | solution.py:103
  747.2 24.4 %collective-permute-start.1 = (bf16[32,16384]{1,0:T(8,128)(2,1)}, bf16[32,16384]{1,0:T(8,128)(2,1)S(1)}, u32[]{:S(2)}, u32[]{:S(2)}) collective-permute-start(bf16[32,16384]{1,0:T(8,128)(2,1)} %convolution_convert_fusion), channel_id=1, source_target_pairs={{0,16},{16,0},{1,17},{17,1},{2,18},{18,2},{3,19},{19,3},{4,20},{20... | collective-permute-start | bytes 3145736 | tf_op jit(solution)/shard_map/ppermute | solution.py:86
  935.3 389.4 %reduce-scatter.9.cloned.1.call-start = ((), (), s32[]{:S(2)}) async-start(), calls=%async_computation.8 | async-start | bytes 35651584 | tf_op jit(solution)/shard_map/reduce_scatter | solution.py:100
  1327.1 1.4 copy-start.1
Sparse Core Ops, SparseCore 0:
  9.6 129.6 all-gather.2
  200.6 52.4 reduce-scatter.6
  258.0 332.7 reduce-scatter.4
  747.3 126.6 all-gather.4
  935.4 52.4 reduce-scatter.10
  992.0 332.6 reduce-scatter.8
